TPU v7x, 32 devices: a whole 2x2x4 slice. The times are simulated.
32 devices in a mesh: seq: 4 (over y, core), dp: 8 (over z, x).
Axes of the slice: x: 2, y: 2, z: 4, core: 2. Of those that a mesh axis runs over, the one named last changes fastest.
Arguments:
- mlp_hidden: bfloat16 [8, 256, 8192], P('dp', None, 'seq'), may hold values from -6 to 6
- encoder_stream: bfloat16 [8, 256, 4096], P('dp', 'seq'), may hold values from -18 to 18
- down_proj: bfloat16 [8192, 4096], P('seq', 'dp'), may hold values from -0.0625 to 0.0625
- final_gain: bfloat16 [4096], replicated, may hold values from 0.25 to 1.75
- kv_proj: bfloat16 [4096, 2, 2048], P('dp', None, 'seq'), may hold values from -0.09375 to 0.09375
- queries: bfloat16 [8, 128, 2048], P('dp', None, 'seq'), may hold values from -640 to 640
- out_proj: bfloat16 [2048, 4096], P('seq'), may hold values from -0.39648438 to 0.39648438
- enc_len: int32 [8], P('dp'), may hold values from 128 to 256, as said below
- dec_pad: int32 [8], P('dp'), may hold values from 0 to 64, as said below
Outputs:
- cross_out: bfloat16 [8, 128, 4096], P('dp', 'seq')
Inputs may be any that keep to these rules, and one draw needn't show every extreme that they name: `enc_len`: at least one filing uses all 256 positions and one uses 256 // 2. `dec_pad`: some filing has no padding and some has 64 padded rows.
All inputs are finite; a program needn't handle non-finite values.
Results may differ from a plain program's by a relative error of at most 0.015.
The roundings to bfloat16 on the way count: a program that leaves them out, or rounds other values in their place, can miss the bound.
Values may be sent and summed in bfloat16 or wider, within the bound.
No kernel may reach another device: no remote copies, remote signals or barrier semaphores. Data moves between devices by JAX's collectives and lax.ppermute only.
A program may use at most 128 MiB of HBM per device.

v0:
```python
import math
import jax
import jax.numpy as jnp
from jax import lax
from jax.sharding import PartitionSpec as P

HD = 256


def normalize(resid, gain_row):
    spread = jnp.mean(resid * resid, axis=-1, keepdims=True)
    return (resid * lax.rsqrt(spread + 1e-06) * gain_row).astype(jnp.bfloat16)


def on_device(
    mlp_hidden, encoder_stream, down_proj, final_gain, kv_proj, queries, out_proj, enc_len, dec_pad
):
    hidden = mlp_hidden[0]
    enc_total = hidden.shape[0]
    gain_row = final_gain.astype(jnp.float32)
    full_down = lax.all_gather(down_proj, "dp", axis=1, tiled=True)
    row_block = hidden
    mlp_out = lax.psum_scatter(
        jnp.dot(row_block, full_down, preferred_element_type=jnp.float32),
        "seq",
        scatter_dimension=0,
        tiled=True,
    )
    normed = normalize(encoder_stream[0].astype(jnp.float32) + mlp_out, gain_row)
    encoded = lax.all_gather(normed, "seq", axis=0, tiled=True)
    heads_here = queries.shape[2] // HD
    kv_width = 2 * heads_here * HD
    weight_piece = lax.all_gather(kv_proj, "dp", axis=0, tiled=True)
    key_value = jnp.dot(
        encoded,
        weight_piece.reshape(weight_piece.shape[0], kv_width),
        preferred_element_type=jnp.float32,
    ).astype(jnp.bfloat16)
    key_value = key_value.reshape(enc_total, 2, heads_here, HD)
    key_rows = key_value[:, 0]
    value_rows = key_value[:, 1]
    dec_rows = queries.shape[1]
    query_rows = queries[0].reshape(dec_rows, heads_here, HD)
    scores = jnp.einsum(
        "qhd,khd->hqk", query_rows, key_rows, preferred_element_type=jnp.float32
    ) / math.sqrt(HD)
    visible = jnp.arange(enc_total, dtype=jnp.int32) < enc_len[0]
    scores = jnp.where(visible[None, None, :], scores, -jnp.inf)
    highest = jnp.max(scores, axis=-1, keepdims=True)
    expo = jnp.exp(scores - highest)
    attention = (expo / jnp.sum(expo, axis=-1, keepdims=True)).astype(jnp.bfloat16)
    attended = jnp.einsum(
        "hqk,khd->qhd", attention, value_rows, preferred_element_type=jnp.float32
    ).astype(jnp.bfloat16)
    row_live = jnp.arange(dec_rows, dtype=jnp.int32) < dec_rows - dec_pad[0]
    attended = jnp.where(row_live[:, None, None], attended, jnp.zeros_like(attended)).reshape(
        dec_rows, heads_here * HD
    )
    row_block = attended
    result = lax.psum_scatter(
        jnp.dot(row_block, out_proj, preferred_element_type=jnp.float32),
        "seq",
        scatter_dimension=0,
        tiled=True,
    )
    return result.astype(jnp.bfloat16)[None]


def solution(mesh):
    placed = (
        P("dp", None, "seq"),
        P("dp", "seq", None),
        P("seq", "dp"),
        P(),
        P("dp", None, "seq"),
        P("dp", None, "seq"),
        P("seq", None),
        P("dp"),
        P("dp"),
    )
    return jax.shard_map(
        on_device, mesh=mesh, in_specs=placed, out_specs=P("dp", "seq", None), check_vma=False
    )
```

profile of v0, /device:TPU:0, one launch (start us, length us, event | category | flops | bytes accessed | tf_op | source)
XLA Modules:
  0.0 494.5 jit_solution(16718448679306863005)
XLA Ops:
  6.5 0.7 all-gather.4.cloned.1.call-update
  7.3 0.0 reduce-scatter.3.cloned.1.call-start
  7.3 232.6 %all-gather.4.cloned.1.call-done = bf16[2048,4096]{1,0:T(8,128)(2,1)} async-done(((bf16[2048,512]{1,0:T(8,128)(2,1)}), bf16[2048,4096]{1,0:T(8,128)(2,1)}) %all-gather.4.cloned.1.call-update) | async-done | bytes 16777232 | tf_op jit(solution)/shard_map/all_gather | solution.py:21
  239.9 10.1 %fusion.6 = f32[256,4096]{1,0:T(8,128)} fusion(bf16[2048,4096]{1,0:T(8,128)(2,1)} %all-gather.4.cloned.1.call-done, bf16[1,256,2048]{2,1,0:T(8,128)(2,1)S(1)} %copy-done), kind=kOutput, calls=%fused_computation.10 | convolution fusion | flops 4294967296 | bytes 22020096 | tf_op jit(solution)/shard_map/dot_general | solution.py:24
  250.0 0.0 all-gather.8.cloned.1.call-start
  250.0 0.7 all-gather.8.cloned.1.call-update
  250.7 0.0 all-gather.6.cloned.1.call-start
  250.8 42.0 %reduce-scatter.3.cloned.1.call-done = f32[64,4096]{1,0:T(8,128)} async-done(((f32[256,4096]{1,0:T(8,128)}), f32[64,4096]{1,0:T(8,128)}) %reduce-scatter.3.cloned.1.call-update) | async-done | bytes 1048592 | tf_op jit(solution)/shard_map/reduce_scatter | solution.py:23
  292.8 1.5 multiply_reduce_fusion
  294.3 2.2 multiply_convert_fusion
  296.5 0.0 reduce-scatter.5.cloned.1.call-start
  297.9 122.2 %all-gather.8.cloned.1.call-done = bf16[4096,2,512]{2,1,0:T(2,128)(2,1)} async-done(((bf16[512,2,512]{2,1,0:T(2,128)(2,1)}), bf16[4096,2,512]{2,1,0:T(2,128)(2,1)}) %all-gather.8.cloned.1.call-update) | async-done | bytes 8388624 | tf_op jit(solution)/shard_map/all_gather | solution.py:33
  420.1 9.3 %copy.21 = bf16[512,8,2,512]{3,1,2,0:T(8,128)(2,1)} copy(bf16[512,8,2,512]{3,2,1,0:T(2,128)(2,1)} %bitcast.32) | data formatting | bytes 16777216
  429.4 13.0 %all-gather.6.cloned.1.call-done = bf16[256,4096]{1,0:T(8,128)(2,1)} async-done(((bf16[64,4096]{1,0:T(8,128)(2,1)}), bf16[256,4096]{1,0:T(8,128)(2,1)}) %all-gather.6.cloned.1.call-update) | async-done | bytes 2097168 | tf_op jit(solution)/shard_map/all_gather | solution.py:30
  442.4 6.3 %convolution_convert_fusion = bf16[256,1024]{1,0:T(8,128)(2,1)S(1)} fusion(bf16[256,4096]{1,0:T(8,128)(2,1)} %all-gather.6.cloned.1.call-done, bf16[4096,1024]{1,0:T(8,128)(2,1)} %bitcast.33), kind=kOutput, calls=%fused_computation.1 | convolution fusion | flops 2147745792 | bytes 11010048 | tf_op jit(solution)/shard_map/dot_general | solution.py:34
  448.8 0.4 reshape.33
  449.2 0.4 fusion.12
  449.5 0.2 fusion.3
  449.8 0.1 fusion.13
  449.9 0.2 copy.19
  450.1 0.3 fusion.5
  450.3 4.3 fusion.14
  454.6 31.6 %reduce-scatter.5.cloned.1.call-done = f32[32,4096]{1,0:T(8,128)} async-done(((f32[128,4096]{1,0:T(8,128)}), f32[32,4096]{1,0:T(8,128)}) %reduce-scatter.5.cloned.1.call-update) | async-done | bytes 524304 | tf_op jit(solution)/shard_map/reduce_scatter | solution.py:60
  486.2 1.8 convert_bitcast_fusion
  (17 shorter events, 0.1 us)
Async XLA Ops:
  6.5 233.4 %copy-start = (bf16[1,256,2048]{2,1,0:T(8,128)(2,1)S(1)}, bf16[1,256,2048]{2,1,0:T(8,128)(2,1)}, u32[]{:S(2)}) copy-start(bf16[1,256,2048]{2,1,0:T(8,128)(2,1)} %param.9) | copy-start | bytes 3145732
  6.5 233.3 %all-gather.4.cloned.1.call-start = ((), (), s32[]{:S(2)}) async-start(), calls=%async_computation.2 | async-start | bytes 18874368 | tf_op jit(solution)/shard_map/all_gather | solution.py:21
  7.3 285.6 %reduce-scatter.3.cloned.1.call-start = ((), (), s32[]{:S(2)}) async-start(), calls=%async_computation.3 | async-start | bytes 5242880 | tf_op jit(solution)/shard_map/reduce_scatter | solution.py:23
  250.0 0.8 copy-start.3
  250.0 42.9 %copy-start.1 = (bf16[1,64,4096]{2,1,0:T(8,128)(2,1)S(1)}, bf16[1,64,4096]{2,1,0:T(8,128)(2,1)}, u32[]{:S(2)}) copy-start(bf16[1,64,4096]{2,1,0:T(8,128)(2,1)} %param.10) | copy-start | bytes 1572868
  250.0 46.6 %copy-start.2 = (bf16[1,128,512]{2,1,0:T(8,128)(2,1)S(1)}, bf16[1,128,512]{2,1,0:T(8,128)(2,1)}, u32[]{:S(2)}) copy-start(bf16[1,128,512]{2,1,0:T(8,128)(2,1)} %param.14) | copy-start | bytes 393220
  250.0 170.1 %all-gather.8.cloned.1.call-start = ((), (), s32[]{:S(2)}) async-start(), calls=%async_computation.5 | async-start | bytes 9437184 | tf_op jit(solution)/shard_map/all_gather | solution.py:33
  250.7 191.7 %all-gather.6.cloned.1.call-start = ((), (), s32[]{:S(2)}) async-start(), calls=%async_computation.4 | async-start | bytes 2621440 | tf_op jit(solution)/shard_map/all_gather | solution.py:30
  296.5 189.7 %reduce-scatter.5.cloned.1.call-start = ((), (), s32[]{:S(2)}) async-start(), calls=%async_computation.6 | async-start | bytes 2621440 | tf_op jit(solution)/shard_map/reduce_scatter | solution.py:60
Sparse Core Ops, SparseCore 0:
  9.4 230.4 all-gather.3
  250.1 42.6 reduce-scatter.2
  295.2 124.9 all-gather.7
  421.6 20.7 all-gather.5
  454.8 31.3 reduce-scatter.4
where the time goes:
time: 495 us
  waiting for transfers between devices  443 us (89%)
  matrix products  21.2 us (4%)
  between operations  14.5 us (3%)
  local copies, waits for them, and re-layouts  10.3 us (2%)
  other arithmetic  5.56 us (1%)
    all_gather x1, waiting for transfers between devices, on_device(): full_down = lax.all_gather(down_proj, 'dp', axis=1, tiled=True)  233 us
    all_gather x1, waiting for transfers between devices, on_device(): weight_piece = lax.all_gather(kv_proj, 'dp', axis=0, tiled=True)  122 us
    reduce_scatter x1, waiting for transfers between devices, on_device(): lax.psum_scatter(jnp.dot(row_block, full_down, preferred_element_type=jnp...  42 us
    reduce_scatter x1, waiting for transfers between devices, on_device(): lax.psum_scatter(jnp.dot(row_block, out_proj, preferred_element_type=jnp....  31.6 us
    all_gather x1, waiting for transfers between devices, on_device(): encoded = lax.all_gather(normed, 'seq', axis=0, tiled=True)  13 us
    dot_general x1, matrix products, on_device(): jnp.dot(row_block, full_down, preferred_element_type=jnp.float32)  10.1 us
  transfers between devices with their start and end apart: 5, of which 5 were waited for; matrix products, arithmetic and copies ran while one was open for 3% of the time, Pallas kernels for 0%

commit v1 on v0

--- a/solution.py
+++ b/solution.py
@@ -5,6 +5,17 @@
 from jax.sharding import PartitionSpec as P
 
 HD = 256
+
+
+def ring_gather(shard, axis, dim):
+    ways = lax.axis_size(axis)
+    pieces = [shard]
+    for far in range(1, ways):
+        pieces.append(
+            lax.ppermute(pieces[far - 1], axis, [(d, (d - 1) % ways) for d in range(ways)])
+        )
+    line = jnp.concatenate(pieces, axis=dim)
+    return jnp.roll(line, lax.axis_index(axis) * shard.shape[dim], axis=dim)
 
 
 def normalize(resid, gain_row):
@@ -18,7 +29,7 @@
     hidden = mlp_hidden[0]
     enc_total = hidden.shape[0]
     gain_row = final_gain.astype(jnp.float32)
-    full_down = lax.all_gather(down_proj, "dp", axis=1, tiled=True)
+    full_down = ring_gather(down_proj, "dp", 1)
     row_block = hidden
     mlp_out = lax.psum_scatter(
         jnp.dot(row_block, full_down, preferred_element_type=jnp.float32),

time: 495 us -> 585 us (1.18)
  local copies, waits for them, and re-layouts: 10.3 us -> 57.7 us
  starting transfers between devices: 0.16 us -> 37.4 us
    ppermute x0 -> x7, waiting for transfers between devices: none -> 282 us  [ring_gather(): lax.ppermute(pieces[far - 1], axis, [(d, (d - 1) % ways) for d in range(w...]
    all_gather x1 -> x0, waiting for transfers between devices: 233 us -> none  [on_device(): full_down = lax.all_gather(down_proj, 'dp', axis=1, tiled=True)]
    all_gather x1, waiting for transfers between devices: 122 us -> 74.7 us  [on_device(): weight_piece = lax.all_gather(kv_proj, 'dp', axis=0, tiled=True)]
    unnamed x5, waiting for transfers between devices: 1.44 us -> 46 us
    reduce_scatter x1 -> x0, waiting for transfers between devices: 42 us -> none  [on_device(): lax.psum_scatter(jnp.dot(row_block, full_down, preferred_element_type=jnp...]
    unnamed x10 -> x48, local copies, waits for them, and re-layouts: 9.51 us -> 51.4 us
    ppermute x0 -> x7, starting transfers between devices: none -> 37 us  [ring_gather(): lax.ppermute(pieces[far - 1], axis, [(d, (d - 1) % ways) for d in range(w...]
  transfers between devices with their start and end apart: 5 -> 11, of which waited for: 5 -> 11; matrix products, arithmetic and copies ran while one was open for 3% -> 5% of each run, Pallas kernels for 0% -> 0%
where the time goes in v1:
time: 585 us; the launch traced here: 584 us
  waiting for transfers between devices  447 us (76%)
  local copies, waits for them, and re-layouts  57.7 us (10%)
  starting transfers between devices  37.4 us (6%)
  matrix products  21.6 us (4%)
  between operations  16.3 us (3%)
    ppermute x7, waiting for transfers between devices, ring_gather(): lax.ppermute(pieces[far - 1], axis, [(d, (d - 1) % ways) for d in range(w...  282 us
    all_gather x1, waiting for transfers between devices, on_device(): weight_piece = lax.all_gather(kv_proj, 'dp', axis=0, tiled=True)  74.7 us
    unnamed x48, local copies, waits for them, and re-layouts  51.4 us
    unnamed x5, waiting for transfers between devices  46 us
    ppermute x7, starting transfers between devices, ring_gather(): lax.ppermute(pieces[far - 1], axis, [(d, (d - 1) % ways) for d in range(w...  37 us
    reduce_scatter x1, waiting for transfers between devices, on_device(): lax.psum_scatter(jnp.dot(row_block, out_proj, preferred_element_type=jnp....  31.6 us
    all_gather x1, waiting for transfers between devices, on_device(): encoded = lax.all_gather(normed, 'seq', axis=0, tiled=True)  12.8 us
  transfers between devices with their start and end apart: 11, of which 11 were waited for; matrix products, arithmetic and copies ran while one was open for 5% of the time, Pallas kernels for 0%

profile of v1, /device:TPU:0, one launch (start us, length us, event | category | flops | bytes accessed | tf_op | source)
XLA Modules:
  0.0 584.1 jit_solution(14453828708154520900)
XLA Ops:
  7.4 6.0 %collective-permute-start = (bf16[2048,512]{1,0:T(8,128)(2,1)}, bf16[2048,512]{1,0:T(8,128)(2,1)S(1)}, u32[]{:S(2)}, u32[]{:S(2)}) collective-permute-start(bf16[2048,512]{1,0:T(8,128)(2,1)} %param.11), channel_id=1, source_target_pairs={{0,7},{1,0},{2,1},{3,2},{4,3},{5,4},{6,5},{7,6},{8,15},{9,8},{10,9... | collective-permute-start | bytes 6291464 | tf_op jit(solution)/shard_map/ppermute | solution.py:15
  13.3 45.2 %collective-permute-done = bf16[2048,512]{1,0:T(8,128)(2,1)S(1)} collective-permute-done((bf16[2048,512]{1,0:T(8,128)(2,1)}, bf16[2048,512]{1,0:T(8,128)(2,1)S(1)}, u32[]{:S(2)}, u32[]{:S(2)}) %collective-permute-start) | collective-permute-done | bytes 2097184 | tf_op jit(solution)/shard_map/ppermute | solution.py:15
  58.6 5.1 collective-permute-start.1
  63.6 44.0 %collective-permute-done.1 = bf16[2048,512]{1,0:T(8,128)(2,1)S(1)} collective-permute-done((bf16[2048,512]{1,0:T(8,128)(2,1)S(1)}, bf16[2048,512]{1,0:T(8,128)(2,1)S(1)}, u32[]{:S(2)}, u32[]{:S(2)}) %collective-permute-start.1) | collective-permute-done | bytes 2097184 | tf_op jit(solution)/shard_map/ppermute | solution.py:15
  109.0 5.2 collective-permute-start.2
  114.1 43.1 %collective-permute-done.2 = bf16[2048,512]{1,0:T(8,128)(2,1)S(1)} collective-permute-done((bf16[2048,512]{1,0:T(8,128)(2,1)S(1)}, bf16[2048,512]{1,0:T(8,128)(2,1)S(1)}, u32[]{:S(2)}, u32[]{:S(2)}) %collective-permute-start.2) | collective-permute-done | bytes 2097184 | tf_op jit(solution)/shard_map/ppermute | solution.py:15
  158.6 5.2 collective-permute-start.3
  163.8 42.2 %collective-permute-done.3 = bf16[2048,512]{1,0:T(8,128)(2,1)S(1)} collective-permute-done((bf16[2048,512]{1,0:T(8,128)(2,1)S(1)}, bf16[2048,512]{1,0:T(8,128)(2,1)S(1)}, u32[]{:S(2)}, u32[]{:S(2)}) %collective-permute-start.3) | collective-permute-done | bytes 2097184 | tf_op jit(solution)/shard_map/ppermute | solution.py:15
  207.3 5.2 collective-permute-start.4
  212.5 41.3 %collective-permute-done.4 = bf16[2048,512]{1,0:T(8,128)(2,1)S(1)} collective-permute-done((bf16[2048,512]{1,0:T(8,128)(2,1)S(1)}, bf16[2048,512]{1,0:T(8,128)(2,1)S(1)}, u32[]{:S(2)}, u32[]{:S(2)}) %collective-permute-start.4) | collective-permute-done | bytes 2097184 | tf_op jit(solution)/shard_map/ppermute | solution.py:15
  255.1 5.2 collective-permute-start.5
  260.2 40.3 %collective-permute-done.5 = bf16[2048,512]{1,0:T(8,128)(2,1)} collective-permute-done((bf16[2048,512]{1,0:T(8,128)(2,1)S(1)}, bf16[2048,512]{1,0:T(8,128)(2,1)}, u32[]{:S(2)}, u32[]{:S(2)}) %collective-permute-start.5) | collective-permute-done | bytes 2097184 | tf_op jit(solution)/shard_map/ppermute | solution.py:15
  300.6 5.3 collective-permute-start.6
  305.9 3.2 constant_dynamic-update-slice_fusion.15
  319.6 26.0 %collective-permute-done.6 = bf16[2048,512]{1,0:T(8,128)(2,1)} collective-permute-done((bf16[2048,512]{1,0:T(8,128)(2,1)}, bf16[2048,512]{1,0:T(8,128)(2,1)}, u32[]{:S(2)}, u32[]{:S(2)}) %collective-permute-start.6) | collective-permute-done | bytes 2097184 | tf_op jit(solution)/shard_map/ppermute | solution.py:15
  363.5 10.4 %fusion.3 = f32[256,4096]{0,1:T(8,128)} fusion(bf16[2048,8192]{1,0:T(8,128)(2,1)} %constant_dynamic-update-slice_fusion, s32[]{:T(128)S(6)} %select_n.28, bf16[1,256,2048]{2,1,0:T(8,128)(2,1)S(1)} %copy-done), kind=kOutput, calls=%fused_computation.3 | convolution fusion | flops 4294967296 | bytes 22020100 | tf_op jit(solution)/shard_map/dot_general | solution.py:35
  373.9 5.7 copy.22
  380.7 45.5 %reduce-scatter.7.cloned.1.call-done = f32[64,4096]{1,0:T(8,128)} async-done(((f32[256,4096]{1,0:T(8,128)}), f32[64,4096]{1,0:T(8,128)}) %reduce-scatter.7.cloned.1.call-update) | async-done | bytes 1048592
  434.1 74.7 %all-gather.5.cloned.1.call-done = bf16[4096,2,512]{2,1,0:T(2,128)(2,1)} async-done(((bf16[512,2,512]{2,1,0:T(2,128)(2,1)}), bf16[4096,2,512]{2,1,0:T(2,128)(2,1)}) %all-gather.5.cloned.1.call-update) | async-done | bytes 8388624 | tf_op jit(solution)/shard_map/all_gather | solution.py:44
  508.8 9.3 %copy.26 = bf16[512,8,2,512]{3,1,2,0:T(8,128)(2,1)} copy(bf16[512,8,2,512]{3,2,1,0:T(2,128)(2,1)} %bitcast.34) | data formatting | bytes 16777216
  518.2 12.8 %all-gather.3.cloned.1.call-done = bf16[256,4096]{1,0:T(8,128)(2,1)} async-done(((bf16[64,4096]{1,0:T(8,128)(2,1)}), bf16[256,4096]{1,0:T(8,128)(2,1)}) %all-gather.3.cloned.1.call-update) | async-done | bytes 2097168 | tf_op jit(solution)/shard_map/all_gather | solution.py:41
  531.0 6.4 %convolution_convert_fusion = bf16[256,1024]{1,0:T(8,128)(2,1)S(1)} fusion(bf16[256,4096]{1,0:T(8,128)(2,1)} %all-gather.3.cloned.1.call-done, bf16[4096,1024]{1,0:T(8,128)(2,1)} %bitcast.35), kind=kOutput, calls=%fused_computation.7 | convolution fusion | flops 2147745792 | bytes 11010048 | tf_op jit(solution)/shard_map/dot_general | solution.py:45
  539.0 4.3 fusion.19
  543.3 31.6 %reduce-scatter.5.cloned.1.call-done = f32[32,4096]{1,0:T(8,128)} async-done(((f32[128,4096]{1,0:T(8,128)}), f32[32,4096]{1,0:T(8,128)}) %reduce-scatter.5.cloned.1.call-update) | async-done | bytes 524304 | tf_op jit(solution)/shard_map/reduce_scatter | solution.py:71
  (68 shorter events, 44.8 us)
Async XLA Ops:
  7.4 356.1 %copy-start = (bf16[1,256,2048]{2,1,0:T(8,128)(2,1)S(1)}, bf16[1,256,2048]{2,1,0:T(8,128)(2,1)}, u32[]{:S(2)}) copy-start(bf16[1,256,2048]{2,1,0:T(8,128)(2,1)} %param.9) | copy-start | bytes 3145732
  7.4 418.8 %reduce-scatter.7.cloned.1.call-start = ((), (), s32[]{:S(2)}) async-start(), calls=%async_computation.5 | async-start | bytes 5242880
  7.4 51.2 %collective-permute-start = (bf16[2048,512]{1,0:T(8,128)(2,1)}, bf16[2048,512]{1,0:T(8,128)(2,1)S(1)}, u32[]{:S(2)}, u32[]{:S(2)}) collective-permute-start(bf16[2048,512]{1,0:T(8,128)(2,1)} %param.11), channel_id=1, source_target_pairs={{0,7},{1,0},{2,1},{3,2},{4,3},{5,4},{6,5},{7,6},{8,15},{9,8},{10,9... | collective-permute-start | bytes 6291464 | tf_op jit(solution)/shard_map/ppermute | solution.py:15
  58.6 49.1 %collective-permute-start.1 = (bf16[2048,512]{1,0:T(8,128)(2,1)S(1)}, bf16[2048,512]{1,0:T(8,128)(2,1)S(1)}, u32[]{:S(2)}, u32[]{:S(2)}) collective-permute-start(bf16[2048,512]{1,0:T(8,128)(2,1)S(1)} %collective-permute-done), channel_id=1, source_target_pairs={{0,7},{1,0},{2,1},{3,2},{4,3},{5,4},{6,5},{7,6},{8,15},{9,8},{10,9... | collective-permute-start | bytes 6291464 | tf_op jit(solution)/shard_map/ppermute | solution.py:15
  107.6 1.3 copy-start.3
  109.0 48.3 %collective-permute-start.2 = (bf16[2048,512]{1,0:T(8,128)(2,1)S(1)}, bf16[2048,512]{1,0:T(8,128)(2,1)S(1)}, u32[]{:S(2)}, u32[]{:S(2)}) collective-permute-start(bf16[2048,512]{1,0:T(8,128)(2,1)S(1)} %collective-permute-done.1), channel_id=1, source_target_pairs={{0,7},{1,0},{2,1},{3,2},{4,3},{5,4},{6,5},{7,6},{8,15},{9,8},{10,9... | collective-permute-start | bytes 6291464 | tf_op jit(solution)/shard_map/ppermute | solution.py:15
  157.2 1.4 copy-start.5
  158.6 47.4 %collective-permute-start.3 = (bf16[2048,512]{1,0:T(8,128)(2,1)S(1)}, bf16[2048,512]{1,0:T(8,128)(2,1)S(1)}, u32[]{:S(2)}, u32[]{:S(2)}) collective-permute-start(bf16[2048,512]{1,0:T(8,128)(2,1)S(1)} %collective-permute-done.2), channel_id=1, source_target_pairs={{0,7},{1,0},{2,1},{3,2},{4,3},{5,4},{6,5},{7,6},{8,15},{9,8},{10,9... | collective-permute-start | bytes 6291464 | tf_op jit(solution)/shard_map/ppermute | solution.py:15
  206.0 1.3 copy-start.7
  207.3 46.4 %collective-permute-start.4 = (bf16[2048,512]{1,0:T(8,128)(2,1)S(1)}, bf16[2048,512]{1,0:T(8,128)(2,1)S(1)}, u32[]{:S(2)}, u32[]{:S(2)}) collective-permute-start(bf16[2048,512]{1,0:T(8,128)(2,1)S(1)} %collective-permute-done.3), channel_id=1, source_target_pairs={{0,7},{1,0},{2,1},{3,2},{4,3},{5,4},{6,5},{7,6},{8,15},{9,8},{10,9... | collective-permute-start | bytes 6291464 | tf_op jit(solution)/shard_map/ppermute | solution.py:15
  255.1 45.5 %collective-permute-start.5 = (bf16[2048,512]{1,0:T(8,128)(2,1)S(1)}, bf16[2048,512]{1,0:T(8,128)(2,1)}, u32[]{:S(2)}, u32[]{:S(2)}) collective-permute-start(bf16[2048,512]{1,0:T(8,128)(2,1)S(1)} %collective-permute-done.4), channel_id=1, source_target_pairs={{0,7},{1,0},{2,1},{3,2},{4,3},{5,4},{6,5},{7,6},{8,15},{9,8},{10,9... | collective-permute-start | bytes 6291464 | tf_op jit(solution)/shard_map/ppermute | solution.py:15
  300.6 45.0 %collective-permute-start.6 = (bf16[2048,512]{1,0:T(8,128)(2,1)}, bf16[2048,512]{1,0:T(8,128)(2,1)}, u32[]{:S(2)}, u32[]{:S(2)}) collective-permute-start(bf16[2048,512]{1,0:T(8,128)(2,1)} %collective-permute-done.5), channel_id=1, source_target_pairs={{0,7},{1,0},{2,1},{3,2},{4,3},{5,4},{6,5},{7,6},{8,15},{9,8},{10,9... | collective-permute-start | bytes 6291464 | tf_op jit(solution)/shard_map/ppermute | solution.py:15
  305.9 4.8 copy-start.4
  305.9 6.2 %copy-start.6 = (bf16[2048,512]{1,0:T(8,128)(2,1)S(1)}, bf16[2048,512]{1,0:T(8,128)(2,1)}, u32[]{:S(2)}) copy-start(bf16[2048,512]{1,0:T(8,128)(2,1)} %copy-done.5) | copy-start | bytes 6291460
  305.9 7.7 %copy-start.8 = (bf16[2048,512]{1,0:T(8,128)(2,1)S(1)}, bf16[2048,512]{1,0:T(8,128)(2,1)}, u32[]{:S(2)}) copy-start(bf16[2048,512]{1,0:T(8,128)(2,1)} %copy-done.7) | copy-start | bytes 6291460
  309.1 6.0 %copy-start.10 = (bf16[2048,512]{1,0:T(8,128)(2,1)S(1)}, bf16[2048,512]{1,0:T(8,128)(2,1)}, u32[]{:S(2)}) copy-start(bf16[2048,512]{1,0:T(8,128)(2,1)} %copy-done.9) | copy-start | bytes 6291460
  313.6 35.0 %copy-start.2 = (bf16[2048,512]{1,0:T(8,128)(2,1)S(1)}, bf16[2048,512]{1,0:T(8,128)(2,1)}, u32[]{:S(2)}) copy-start(bf16[2048,512]{1,0:T(8,128)(2,1)} %param.11) | copy-start | bytes 6291460
  373.9 6.3 %copy-start.11 = (bf16[1,64,4096]{2,1,0:T(8,128)(2,1)S(1)}, bf16[1,64,4096]{2,1,0:T(8,128)(2,1)}, u32[]{:S(2)}) copy-start(bf16[1,64,4096]{2,1,0:T(8,128)(2,1)} %param.10) | copy-start | bytes 1572868
  373.9 6.8 %copy-start.13 = (bf16[4096]{0:T(1024)(128)(2,1)S(1)}, bf16[4096]{0:T(1024)(128)(2,1)}, u32[]{:S(2)}) copy-start(bf16[4096]{0:T(1024)(128)(2,1)} %param.12) | copy-start | bytes 24580
  379.6 53.2 %copy-start.12 = (bf16[1,128,512]{2,1,0:T(8,128)(2,1)S(1)}, bf16[1,128,512]{2,1,0:T(8,128)(2,1)}, u32[]{:S(2)}) copy-start(bf16[1,128,512]{2,1,0:T(8,128)(2,1)} %param.14) | copy-start | bytes 393220
  379.6 129.3 %all-gather.5.cloned.1.call-start = ((), (), s32[]{:S(2)}) async-start(), calls=%async_computation.3 | async-start | bytes 9437184 | tf_op jit(solution)/shard_map/all_gather | solution.py:44
  380.2 150.8 %all-gather.3.cloned.1.call-start = ((), (), s32[]{:S(2)}) async-start(), calls=%async_computation.2 | async-start | bytes 2621440 | tf_op jit(solution)/shard_map/all_gather | solution.py:41
  432.5 142.4 %reduce-scatter.5.cloned.1.call-start = ((), (), s32[]{:S(2)}) async-start(), calls=%async_computation.4 | async-start | bytes 2621440 | tf_op jit(solution)/shard_map/reduce_scatter | solution.py:71
  531.0 45.7 %copy-start.1 = (bf16[1,256,2048]{2,1,0:T(8,128)(2,1)S(1)}, bf16[1,256,2048]{2,1,0:T(8,128)(2,1)}, u32[]{:S(2)}) copy-start(bf16[1,256,2048]{2,1,0:T(8,128)(2,1)} %param.9) | copy-start | bytes 3145732
  (1 other events, 1.3 us)
Sparse Core Ops, SparseCore 0:
  379.7 46.4 reduce-scatter.6
  543.4 31.4 reduce-scatter.4
Sparse Core Ops, SparseCore 1:
  382.4 126.4 all-gather.4
  510.3 20.6 all-gather.2
